TPU v7x, 256 devices: a whole 4x4x8 slice. The times are simulated.
256 devices in a mesh: gx: 8 (over y, core), gy: 32 (over x, z).
Axes of the slice: x: 4, y: 4, z: 8, core: 2. Of those that a mesh axis runs over, the one named last changes fastest.
Arguments:
- flow_field: float32 [16, 256, 256, 128], P(None, 'gx', 'gy'), may hold values from -6 to 6
- cotangent: float32 [16, 256, 256, 128], P(None, 'gx', 'gy'), may hold values from -6 to 6
- mode_weights: float32 [4, 16, 16, 256], replicated, may hold values from -3 to 3
- point_weights: float32 [16, 16], replicated, may hold values from -1.5 to 1.5
- point_bias: float32 [16], replicated, may hold values from -3 to 3
Outputs:
- output_field: float32 [16, 256, 256, 128], P(None, 'gx', 'gy')
- grad_field: float32 [16, 256, 256, 128], P(None, 'gx', 'gy')
- grad_modes: float32 [4, 16, 16, 256], replicated
- grad_point: float32 [16, 16], replicated
- grad_bias: float32 [16], replicated
All inputs are finite; a program needn't handle non-finite values.
Results may differ from a plain program's by a relative error of at most 0.00024.
Values sent between devices are 32-bit elements; how exact they have to be, the bound alone decides.
No kernel may reach another device: no remote copies, remote signals or barrier semaphores. Data moves between devices by JAX's collectives and lax.ppermute only.
A program may use at most 128 MiB of HBM per device.

v0:
```python
import math
import jax
import jax.numpy as jnp
from jax import lax
from jax.sharding import PartitionSpec as P

LOW_PASS = [
    0.23037781330885523,
    0.7148465705525415,
    0.6308807679295904,
    -0.02798376941698385,
    -0.18703481171888114,
    0.030841381835986965,
    0.032883011666982945,
    -0.010597401784997278,
]
HIGH_PASS = [(-1) ** position * LOW_PASS[7 - position] for position in range(8)]
GELU_SCALE = 0.7978845608028654
GELU_CUBE = 0.044715


def from_behind(value, axis, by):
    devices = lax.axis_size(axis)
    return lax.ppermute(value, axis, [(i, (i + by) % devices) for i in range(devices)])


def filter_table(filter_taps, out_count, in_count, periodic):
    row_index = lax.broadcasted_iota(jnp.int32, (out_count, in_count), 0)
    col_index = lax.broadcasted_iota(jnp.int32, (out_count, in_count), 1)
    offset = col_index - 2 * row_index
    if periodic:
        offset = offset % in_count
    matrix = jnp.zeros((out_count, in_count), jnp.float32)
    for position in range(8):
        matrix = matrix + filter_taps[position] * (offset == position).astype(jnp.float32)
    return matrix


def lifted_table(filter_taps, out_count, in_count):
    row_index = lax.broadcasted_iota(jnp.int32, (out_count, in_count), 0)
    col_index = lax.broadcasted_iota(jnp.int32, (out_count, in_count), 1)
    offset = row_index - 2 * col_index + 6
    matrix = jnp.zeros((out_count, in_count), jnp.float32)
    for position in range(8):
        matrix = matrix + filter_taps[position] * (offset == position).astype(jnp.float32)
    return matrix


def along_x(matrix, signal):
    return jnp.einsum("kr,arys->akys", matrix, signal, precision=lax.Precision.HIGHEST)


def along_y(matrix, signal):
    return jnp.einsum("kr,axrs->axks", matrix, signal, precision=lax.Precision.HIGHEST)


def plane_x(matrix, signal):
    return jnp.einsum("kr,ary->aky", matrix, signal, precision=lax.Precision.HIGHEST)


def plane_y(matrix, signal):
    return jnp.einsum("kr,axr->axk", matrix, signal, precision=lax.Precision.HIGHEST)


def to_lanes(signal):
    channels, extent_x, extent_y, planes = signal.shape
    return jnp.transpose(signal, (0, 3, 1, 2)).reshape(channels * planes, extent_x, extent_y)


def from_lanes(signal, channels):
    stacked, extent_x, extent_y = signal.shape
    return jnp.transpose(
        signal.reshape(channels, stacked // channels, extent_x, extent_y), (0, 2, 3, 1)
    )


def four_bands(signal):
    extent_x, extent_y = (signal.shape[1], signal.shape[2])
    low_x = plane_x(filter_table(LOW_PASS, extent_x // 2, extent_x, True), signal)
    high_x = plane_x(filter_table(HIGH_PASS, extent_x // 2, extent_x, True), signal)
    low_y = filter_table(LOW_PASS, extent_y // 2, extent_y, True)
    high_y = filter_table(HIGH_PASS, extent_y // 2, extent_y, True)
    return jnp.stack(
        [
            plane_y(low_y, low_x),
            plane_y(low_y, high_x),
            plane_y(high_y, low_x),
            plane_y(high_y, high_x),
        ]
    )


def join_bands(changes):
    modes_x, modes_y = (changes.shape[2], changes.shape[3])
    low_x = filter_table(LOW_PASS, modes_x, 2 * modes_x, True).T
    high_x = filter_table(HIGH_PASS, modes_x, 2 * modes_x, True).T
    low_y = filter_table(LOW_PASS, modes_y, 2 * modes_y, True).T
    high_y = filter_table(HIGH_PASS, modes_y, 2 * modes_y, True).T
    from_low = plane_y(low_y, changes[0]) + plane_y(high_y, changes[2])
    from_high = plane_y(low_y, changes[1]) + plane_y(high_y, changes[3])
    return plane_x(low_x, from_low) + plane_x(high_x, from_high)


def gelu_parts(signal):
    tangent = jnp.tanh(GELU_SCALE * (signal + GELU_CUBE * signal * signal * signal))
    activated = 0.5 * signal * (1.0 + tangent)
    gelu_slope = 0.5 * (1.0 + tangent) + 0.5 * signal * (1.0 - tangent * tangent) * GELU_SCALE * (
        1.0 + 3.0 * GELU_CUBE * signal * signal
    )
    return (activated, gelu_slope)


def wave_block(signal, weights_grid, transposed):
    x_index = lax.axis_index("gx")
    channels = signal.shape[0]
    extent_x, extent_y = (signal.shape[1], signal.shape[2])
    margin = from_behind(signal[:, :6], "gx", -1)
    halved = along_x(
        filter_table(LOW_PASS, extent_x // 2, extent_x + 6, False),
        jnp.concatenate([signal, margin], 1),
    )
    margin = from_behind(halved[:, :, :6], "gy", -1)
    level_one = along_y(
        filter_table(LOW_PASS, extent_y // 2, extent_y + 6, False),
        jnp.concatenate([halved, margin], 2),
    )
    level_one = to_lanes(lax.all_to_all(level_one, "gy", split_axis=3, concat_axis=2, tiled=True))
    rows_one, cols_one = (level_one.shape[1], level_one.shape[2])
    margin = from_behind(level_one[:, :6], "gx", -1)
    level_two = plane_x(
        filter_table(LOW_PASS, rows_one // 2, rows_one + 6, False),
        jnp.concatenate([level_one, margin], 1),
    )
    level_two = plane_y(filter_table(LOW_PASS, cols_one // 2, cols_one, True), level_two)
    rows_two, cols_two = (level_two.shape[1], level_two.shape[2])
    margin = from_behind(level_two[:, :6], "gx", -1)
    level_three = plane_x(
        filter_table(LOW_PASS, rows_two // 2, rows_two + 6, False),
        jnp.concatenate([level_two, margin], 1),
    )
    level_three = plane_y(filter_table(LOW_PASS, cols_two // 2, cols_two, True), level_three)
    gathered = lax.all_gather(level_three, "gx", axis=1, tiled=True)
    wave_bands = four_bands(gathered)
    stacked, modes_x, modes_y = (wave_bands.shape[1], wave_bands.shape[2], wave_bands.shape[3])
    split_bands = wave_bands.reshape(4, channels, stacked // channels, modes_x, modes_y)
    if transposed:
        mixed_bands = jnp.einsum(
            "bozxy,bioxy->bizxy", split_bands, weights_grid, precision=lax.Precision.HIGHEST
        )
    else:
        mixed_bands = jnp.einsum(
            "bizxy,bioxy->bozxy", split_bands, weights_grid, precision=lax.Precision.HIGHEST
        )
    delta_three = join_bands((mixed_bands - split_bands).reshape(4, stacked, modes_x, modes_y))
    own_rows = rows_two // 2
    own_part = lax.dynamic_slice_in_dim(delta_three, x_index * own_rows, own_rows, 1)
    margin = from_behind(own_part[:, own_rows - 3 :], "gx", 1)
    delta_two = plane_x(
        lifted_table(LOW_PASS, 2 * own_rows, own_rows + 3), jnp.concatenate([margin, own_part], 1)
    )
    cols_three = own_part.shape[2]
    delta_two = plane_y(filter_table(LOW_PASS, cols_three, 2 * cols_three, True).T, delta_two)
    margin = from_behind(delta_two[:, rows_two - 3 :], "gx", 1)
    delta_one = plane_x(
        lifted_table(LOW_PASS, 2 * rows_two, rows_two + 3), jnp.concatenate([margin, delta_two], 1)
    )
    delta_one = plane_y(filter_table(LOW_PASS, cols_two, 2 * cols_two, True).T, delta_one)
    returned = lax.all_to_all(
        from_lanes(delta_one, channels), "gy", split_axis=2, concat_axis=3, tiled=True
    )
    rows_back = returned.shape[1]
    margin = from_behind(returned[:, rows_back - 3 :], "gx", 1)
    widened = along_x(
        lifted_table(LOW_PASS, 2 * rows_back, rows_back + 3), jnp.concatenate([margin, returned], 1)
    )
    cols_back = widened.shape[2]
    margin = from_behind(widened[:, :, cols_back - 3 :], "gy", 1)
    delta_zero = along_y(
        lifted_table(LOW_PASS, 2 * cols_back, cols_back + 3), jnp.concatenate([margin, widened], 2)
    )
    return (signal + delta_zero, split_bands)


def local(flow_field, cotangent, mode_weights, point_weights, point_bias):
    channels = flow_field.shape[0]
    modes_x = flow_field.shape[1] * lax.axis_size("gx") // 16
    modes_y = flow_field.shape[2] * lax.axis_size("gy") // 16
    weights_grid = mode_weights.reshape(4, channels, channels, modes_x, modes_y)
    spectral_flow, bands_flow = wave_block(flow_field, weights_grid, False)
    pointwise = jnp.einsum(
        "io,ixys->oxys", point_weights, flow_field, precision=lax.Precision.HIGHEST
    )
    before_gelu = spectral_flow + pointwise + point_bias[:, None, None, None]
    output_field, gelu_slope = gelu_parts(before_gelu)
    grad_inner = cotangent * gelu_slope
    spectral_grad, bands_grad = wave_block(grad_inner, weights_grid, True)
    point_back = jnp.einsum(
        "io,oxys->ixys", point_weights, grad_inner, precision=lax.Precision.HIGHEST
    )
    grad_field = spectral_grad + point_back
    mode_local = jnp.einsum(
        "bizxy,bozxy->bioxy", bands_flow, bands_grad, precision=lax.Precision.HIGHEST
    )
    mode_local = mode_local.reshape(4, channels, channels, modes_x * modes_y)
    mode_total = lax.psum(mode_local, "gy")
    point_local = jnp.einsum(
        "ixys,oxys->io", flow_field, grad_inner, precision=lax.Precision.HIGHEST
    )
    bias_local = jnp.sum(grad_inner, axis=(1, 2, 3))
    point_total, bias_total = lax.psum((point_local, bias_local), ("gx", "gy"))
    plane_total = flow_field.shape[3]
    cell_count = (
        plane_total
        * flow_field.shape[1]
        * flow_field.shape[2]
        * lax.axis_size("gx")
        * lax.axis_size("gy")
    )
    grad_modes = mode_total / math.sqrt(plane_total)
    grad_point = point_total / math.sqrt(cell_count)
    grad_bias = bias_total / math.sqrt(cell_count)
    return (output_field, grad_field, grad_modes, grad_point, grad_bias)


def solution(mesh):
    in_specs = (P(None, "gx", "gy", None), P(None, "gx", "gy", None), P(), P(), P())
    out_specs = (P(None, "gx", "gy", None), P(None, "gx", "gy", None), P(), P(), P())
    return jax.shard_map(local, mesh=mesh, in_specs=in_specs, out_specs=out_specs, check_vma=False)
```

profile of v0, /device:TPU:8, one launch (start us, length us, event | category | flops | bytes accessed | tf_op | source)
XLA Modules:
  0.0 609.2 jit_solution(3356555167298708479)
XLA Ops:
  9.3 6.7 %collective-permute-done = f32[16,6,8,128]{3,1,2,0:T(8,128)S(1)} collective-permute-done((f32[16,6,8,128]{3,1,2,0:T(8,128)S(1)}, f32[16,6,8,128]{3,1,2,0:T(8,128)S(1)}, u32[]{:S(2)}, u32[]{:S(2)}) %collective-permute-start) | collective-permute-done | bytes 393248 | tf_op jit(solution)/shard_map/ppermute | solution.py:24
  17.9 8.1 %collective-permute-start.1 = (f32[16,16,6,128]{3,1,2,0:T(8,128)S(1)}, f32[16,16,6,128]{3,1,2,0:T(8,128)S(1)}, u32[]{:S(2)}, u32[]{:S(2)}) collective-permute-start(f32[16,16,6,128]{3,1,2,0:T(8,128)S(1)} %slice.105), channel_id=1, source_target_pairs={{0,31},{1,0},{2,1},{3,2},{4,3},{5,4},{6,5},{7,6},{8,7},{9,8},{10,9... | collective-permute-start | bytes 2359304 | tf_op jit(solution)/shard_map/ppermute | solution.py:24
  26.0 17.1 %collective-permute-done.1 = f32[16,16,6,128]{3,1,2,0:T(8,128)S(1)} collective-permute-done((f32[16,16,6,128]{3,1,2,0:T(8,128)S(1)}, f32[16,16,6,128]{3,1,2,0:T(8,128)S(1)}, u32[]{:S(2)}, u32[]{:S(2)}) %collective-permute-start.1) | collective-permute-done | bytes 786464 | tf_op jit(solution)/shard_map/ppermute | solution.py:24
  45.4 4.4 copy.209
  49.8 4.3 reshape.86
  54.1 7.6 %all-to-all-start = ((f32[32,1,4096]{2,1,0:T(1,128)}), f32[32,1,4096]{2,1,0:T(1,128)S(1)}, u32[]{:S(2)}, u32[]{:S(2)}) async-start(f32[32,1,4096]{2,1,0:T(1,128)} %reshape.86), calls=%async_computation | async-start | bytes 1048576 | tf_op jit(solution)/shard_map/all_to_all | solution.py:127
  61.7 6.2 %copy.304 = f32[4,16,16,256]{2,1,3,0:T(8,128)} copy(f32[4,16,16,256]{3,2,1,0:T(8,128)S(1)} %copy-done.4) | data formatting | bytes 2097152 | tf_op jit(solution)/shard_map/reshape | solution.py:188
  68.0 11.4 %all-to-all-done = f32[32,1,4096]{2,1,0:T(1,128)S(1)} async-done(((f32[32,1,4096]{2,1,0:T(1,128)}), f32[32,1,4096]{2,1,0:T(1,128)S(1)}, u32[]{:S(2)}, u32[]{:S(2)}) %all-to-all-start) | async-done | bytes 524320 | tf_op jit(solution)/shard_map/all_to_all | solution.py:127
  84.6 4.8 copy.211
  89.4 3.7 copy.212
  93.2 3.9 collective-permute-done.2
  100.1 3.9 collective-permute-done.3
  105.0 14.3 %all_gather.6 = f32[64,32,32]{0,2,1:T(8,128)S(1)} all-gather(f32[64,4,32]{0,2,1:T(8,128)S(1)} %fusion.123), channel_id=1, replica_groups=mesh['gx'=8,'gy'=32] {'gx'}, dimensions={1}, use_global_device_ids=true | all-gather | bytes 294912 | tf_op jit(solution)/shard_map/all_gather | solution.py:142
  125.7 14.9 %bitcast_subtract_fusion.1 = f32[4,16,4,16,16]{1,2,4,3,0:T(4,128)S(1)} fusion(f32[4,16,16,16,16]{2,1,4,3,0:T(8,128)} %bitcast.264, f32[1,16,4,16,16]{1,2,4,3,0:T(4,128)S(1)} %copy.227, f32[1,16,4,16,16]{1,2,4,3,0:T(4,128)S(1)} %copy.226, f32[1,16,4,16,16]{1,2,4,3,0:T(4,128)S(1)} %copy.225, f32[1,16,4,16,16]{1,2,4,3,0:T(4,128)S(1)} %copy.224), kind=kOutput, calls=%fused_computation.23 | convolution fusion | flops 13041664 | bytes 1572864 | tf_op jit(solution)/shard_map/bizxy,bioxy->bozxy/dot_general | solution.py:151
  150.9 4.8 collective-permute-done.4
  156.7 4.0 collective-permute-done.5
  162.3 4.4 copy.241
  166.7 4.8 bitcast_bitcast_fusion.1
  175.0 22.0 %all_to_all.72 = f32[32,1,4096]{2,1,0:T(1,128)S(1)} all-to-all(f32[32,1,4096]{2,1,0:T(1,128)S(1)} %reshape.88), channel_id=1, replica_groups=mesh['gx'=8,'gy'=32] {'gy'}, dimensions={0} | all-to-all | bytes 1048576 | tf_op jit(solution)/shard_map/all_to_all | solution.py:168
  201.8 4.7 copy.242
  209.4 4.4 collective-permute-done.6
  220.1 15.0 %collective-permute-done.7 = f32[16,32,3,128]{3,1,2,0:T(8,128)S(1)} collective-permute-done((f32[16,32,3,128]{3,1,2,0:T(8,128)S(1)}, f32[16,32,3,128]{3,1,2,0:T(8,128)S(1)}, u32[]{:S(2)}, u32[]{:S(2)}) %collective-permute-start.7) | collective-permute-done | bytes 786464 | tf_op jit(solution)/shard_map/ppermute | solution.py:24
  235.3 6.6 %fusion.1133 = (f32[16]{0:T(128)}, f32[16,32,8,128]{3,2,1,0:T(8,128)S(1)}, f32[16,32,8,128]{3,2,1,0:T(8,128)}) fusion(f32[16,32,8,128]{3,2,1,0:T(8,128)S(1)} %copy-done.20, f32[16]{0:T(128)S(1)} %copy-done.21, f32[16,32,8,128]{3,0,2,1:T(8,128)S(1)} %fusion.27, f32[16,32,8,128]{3,2,1,0:T(8,128)S(1)} %copy-done.1, s32[7]{0:T(128)S(1)} %iota_multiply_fusion.2, ...), kind=kOutput, calls=%fused_computation.1198 | convolution fusion | flops 56100200 | bytes 12320924 | tf_op jit(solution)/shard_map/kr,axrs->axks/dot_general | solution.py:54
  241.9 5.3 collective-permute-done.8
  249.6 19.6 %collective-permute-done.9 = f32[16,16,6,128]{3,1,2,0:T(8,128)S(1)} collective-permute-done((f32[16,16,6,128]{3,1,2,0:T(8,128)S(1)}, f32[16,16,6,128]{3,1,2,0:T(8,128)S(1)}, u32[]{:S(2)}, u32[]{:S(2)}) %collective-permute-start.9) | collective-permute-done | bytes 786464 | tf_op jit(solution)/shard_map/ppermute | solution.py:24
  271.5 4.4 copy.251
  279.4 19.5 %all_to_all.73 = f32[32,1,4096]{2,1,0:T(1,128)S(1)} all-to-all(f32[32,1,4096]{2,1,0:T(1,128)S(1)} %reshape.90), channel_id=1, replica_groups=mesh['gx'=8,'gy'=32] {'gy'}, dimensions={0} | all-to-all | bytes 1048576 | tf_op jit(solution)/shard_map/all_to_all | solution.py:127
  303.6 4.8 copy.253
  308.4 3.7 copy.254
  312.2 3.9 collective-permute-done.10
  319.1 5.1 collective-permute-done.11
  325.1 17.3 %all_gather.7 = f32[64,32,32]{0,2,1:T(8,128)S(1)} all-gather(f32[64,4,32]{0,2,1:T(8,128)S(1)} %fusion.119), channel_id=1, replica_groups=mesh['gx'=8,'gy'=32] {'gx'}, dimensions={1}, use_global_device_ids=true | all-gather | bytes 294912 | tf_op jit(solution)/shard_map/all_gather | solution.py:142
  350.4 18.2 %bitcast_subtract_fusion = f32[4,16,4,16,16]{1,2,4,3,0:T(4,128)S(1)} fusion(f32[4,16,16,16,16]{2,1,4,3,0:T(8,128)} %bitcast.265, f32[1,16,4,16,16]{1,2,4,3,0:T(4,128)} %copy.269, f32[1,16,4,16,16]{1,2,4,3,0:T(4,128)} %copy.268, f32[1,16,4,16,16]{1,2,4,3,0:T(4,128)} %copy.267, f32[1,16,4,16,16]{1,2,4,3,0:T(4,128)S(1)} %copy.266), kind=kOutput, calls=%fused_computation.19 | convolution fusion | flops 13041664 | bytes 1572864 | tf_op jit(solution)/shard_map/bozxy,bioxy->bizxy/dot_general | solution.py:147
  384.9 4.8 collective-permute-done.12
  390.7 4.0 collective-permute-done.13
  396.3 4.4 copy.283
  400.7 4.7 bitcast_bitcast_fusion
  405.5 4.2 reshape.92
  409.7 5.7 all-to-all-start.3
  415.5 17.6 %fusion.86 = f32[4,16,16,16,16]{4,3,2,1,0:T(8,128)} fusion(f32[1,16,4,16,16]{1,2,4,3,0:T(4,128)} %copy.269, f32[1,16,4,16,16]{1,2,4,3,0:T(4,128)} %copy.268, f32[1,16,4,16,16]{1,2,4,3,0:T(4,128)} %copy.267, f32[1,16,4,16,16]{1,2,4,3,0:T(4,128)} %copy-done.10, f32[1,16,4,16,16]{1,2,4,3,0:T(4,128)} %copy-done.9, f32[1,16,4,16,16]{1,2,4,3,0:T(4,128)} %copy-done.7, ...), kind=kOutput, calls=%fused_computation.106 | convolution fusion | flops 12976128 | bytes 1572864 | tf_op jit(solution)/shard_map/bizxy,bozxy->bioxy/dot_general | solution.py:201
  433.0 7.7 %copy.290 = f32[4,16,16,256]{3,2,1,0:T(8,128)} copy(f32[4,16,16,256]{1,2,3,0:T(8,128)} %bitcast.266) | data formatting | bytes 2097152 | tf_op jit(solution)/shard_map/reshape | solution.py:204
  440.8 6.3 %fusion.45 = f32[16,16]{0,1:T(8,128)S(1)} fusion(f32[16,32,8,128]{3,2,1,0:T(8,128)} %param.5, f32[16,32,8,128]{3,2,1,0:T(8,128)S(1)} %get-tuple-element.28), kind=kOutput, calls=%fused_computation.66 | convolution fusion | flops 100663296 | bytes 4195328 | tf_op jit(solution)/shard_map/ixys,oxys->io/dot_general | solution.py:206
  447.1 77.5 %all-reduce = (f32[16,16]{0,1:T(8,128)S(1)}, f32[16]{0:T(128)S(1)}) all-reduce(f32[16,16]{0,1:T(8,128)S(1)} %fusion.45, f32[16]{0:T(128)S(1)} %copy-done.19), channel_id=1, replica_groups=mesh['gx'=8,'gy'=32] {'gx','gy'}, use_global_device_ids=true, to_apply=%region_1.2 | all-reduce | flops 272 | bytes 2176 | tf_op jit(solution)/shard_map/psum | solution.py:210
  529.3 4.8 copy.284
  537.7 4.1 collective-permute-done.14
  547.0 4.4 fusion.24
  551.4 41.4 %all-reduce.3.cloned.1.call-done = f32[4,16,16,256]{3,2,1,0:T(8,128)} async-done(((f32[4,16,16,256]{3,2,1,0:T(8,128)}), f32[4,16,16,256]{3,2,1,0:T(8,128)}) %all-reduce.3.cloned.1.call-update) | async-done | bytes 1048592 | tf_op jit(solution)/shard_map/psum | solution.py:205
  596.9 5.2 bitcast_add_fusion
  (185 shorter events, 113.2 us)
Async XLA Ops:
  7.2 210.0 %copy-start = (f32[16,16]{1,0:T(8,128)S(1)}, f32[16,16]{1,0:T(8,128)}, u32[]{:S(2)}) copy-start(f32[16,16]{1,0:T(8,128)} %param.8) | copy-start | bytes 3076
  9.2 6.7 %collective-permute-start = (f32[16,6,8,128]{3,1,2,0:T(8,128)S(1)}, f32[16,6,8,128]{3,1,2,0:T(8,128)S(1)}, u32[]{:S(2)}, u32[]{:S(2)}) collective-permute-start(f32[16,6,8,128]{3,1,2,0:T(8,128)S(1)} %slice.104), channel_id=1, source_target_pairs={{0,224},{32,0},{64,32},{96,64},{128,96},{160,128},{192,160},{224,1... | collective-permute-start | bytes 1179656 | tf_op jit(solution)/shard_map/ppermute | solution.py:24
  17.9 25.2 %collective-permute-start.1 = (f32[16,16,6,128]{3,1,2,0:T(8,128)S(1)}, f32[16,16,6,128]{3,1,2,0:T(8,128)S(1)}, u32[]{:S(2)}, u32[]{:S(2)}) collective-permute-start(f32[16,16,6,128]{3,1,2,0:T(8,128)S(1)} %slice.105), channel_id=1, source_target_pairs={{0,31},{1,0},{2,1},{3,2},{4,3},{5,4},{6,5},{7,6},{8,7},{9,8},{10,9... | collective-permute-start | bytes 2359304 | tf_op jit(solution)/shard_map/ppermute | solution.py:24
  49.8 12.0 %copy-start.4 = (f32[4,16,16,256]{3,2,1,0:T(8,128)S(1)}, f32[4,16,16,256]{3,2,1,0:T(8,128)}, u32[]{:S(2)}) copy-start(f32[4,16,16,256]{3,2,1,0:T(8,128)} %param.7) | copy-start | bytes 3145732
  54.1 25.3 %all-to-all-start = ((f32[32,1,4096]{2,1,0:T(1,128)}), f32[32,1,4096]{2,1,0:T(1,128)S(1)}, u32[]{:S(2)}, u32[]{:S(2)}) async-start(f32[32,1,4096]{2,1,0:T(1,128)} %reshape.86), calls=%async_computation | async-start | bytes 1048576 | tf_op jit(solution)/shard_map/all_to_all | solution.py:127
  93.2 3.9 collective-permute-start.2
  98.2 5.8 collective-permute-start.3
  100.1 224.6 %copy-start.15 = (s32[32]{0:T(128)}, s32[32]{0:T(128)S(1)}, u32[]{:S(2)}) copy-start(s32[32]{0:T(128)S(1)} %iota_multiply_fusion.3) | copy-start | bytes 388
  122.9 2.0 copy-start.5
  123.5 1.3 copy-start.7
  124.2 0.8 copy-start.8
  124.8 0.8 copy-start.9
  150.8 5.0 collective-permute-start.4
  150.9 84.3 %copy-start.11 = (s32[7]{0:T(128)}, s32[7]{0:T(128)S(1)}, u32[]{:S(2)}) copy-start(s32[7]{0:T(128)S(1)} %iota_multiply_fusion.2) | copy-start | bytes 88
  156.7 4.1 collective-permute-start.5
  156.7 10.0 %copy-start.17 = (s32[11]{0:T(128)}, s32[11]{0:T(128)S(1)}, u32[]{:S(2)}) copy-start(s32[11]{0:T(128)S(1)} %iota_multiply_fusion.1) | copy-start | bytes 136
  209.3 7.9 %copy-start.1 = (f32[16,32,8,128]{3,2,1,0:T(8,128)S(1)}, f32[16,32,8,128]{3,2,1,0:T(8,128)}, u32[]{:S(2)}) copy-start(f32[16,32,8,128]{3,2,1,0:T(8,128)} %param.5) | copy-start | bytes 6291460
  209.3 4.4 collective-permute-start.6
  209.4 10.7 %copy-start.13 = (s32[19]{0:T(128)}, s32[19]{0:T(128)S(1)}, u32[]{:S(2)}) copy-start(s32[19]{0:T(128)S(1)} %iota_multiply_fusion) | copy-start | bytes 232
  214.9 20.2 %collective-permute-start.7 = (f32[16,32,3,128]{3,1,2,0:T(8,128)S(1)}, f32[16,32,3,128]{3,1,2,0:T(8,128)S(1)}, u32[]{:S(2)}, u32[]{:S(2)}) collective-permute-start(f32[16,32,3,128]{3,1,2,0:T(8,128)S(1)} %slice.115), channel_id=1, source_target_pairs={{0,1},{1,2},{2,3},{3,4},{4,5},{5,6},{6,7},{7,8},{8,9},{9,10},{10,1... | collective-permute-start | bytes 2359304 | tf_op jit(solution)/shard_map/ppermute | solution.py:24
  220.0 15.2 %copy-start.20 = (f32[16,32,8,128]{3,2,1,0:T(8,128)S(1)}, f32[16,32,8,128]{3,2,1,0:T(8,128)}, u32[]{:S(2)}) copy-start(f32[16,32,8,128]{3,2,1,0:T(8,128)} %param.6) | copy-start | bytes 6291460
  220.0 15.2 %copy-start.21 = (f32[16]{0:T(128)S(1)}, f32[16]{0:T(128)}, u32[]{:S(2)}) copy-start(f32[16]{0:T(128)} %param.9) | copy-start | bytes 196
  241.9 5.3 collective-permute-start.8
  249.5 19.7 %collective-permute-start.9 = (f32[16,16,6,128]{3,1,2,0:T(8,128)S(1)}, f32[16,16,6,128]{3,1,2,0:T(8,128)S(1)}, u32[]{:S(2)}, u32[]{:S(2)}) collective-permute-start(f32[16,16,6,128]{3,1,2,0:T(8,128)S(1)} %slice.117), channel_id=1, source_target_pairs={{0,31},{1,0},{2,1},{3,2},{4,3},{5,4},{6,5},{7,6},{8,7},{9,8},{10,9... | collective-permute-start | bytes 2359304 | tf_op jit(solution)/shard_map/ppermute | solution.py:24
  312.2 3.9 collective-permute-start.10
  317.2 7.0 %collective-permute-start.11 = (f32[64,6,64]{2,1,0:T(8,128)S(1)}, f32[64,6,64]{2,1,0:T(8,128)S(1)}, u32[]{:S(2)}, u32[]{:S(2)}) collective-permute-start(f32[64,6,64]{2,1,0:T(8,128)S(1)} %bitcast.290), channel_id=1, source_target_pairs={{0,224},{32,0},{64,32},{96,64},{128,96},{160,128},{192,160},{224,1... | collective-permute-start | bytes 294920 | tf_op jit(solution)/shard_map/ppermute | solution.py:24
  346.1 4.4 copy-start.10
  379.3 10.5 %copy-start.12 = (s32[7]{0:T(128)S(1)}, s32[7]{0:T(128)}, u32[]{:S(2)}) copy-start(s32[7]{0:T(128)} %copy-done.11) | copy-start | bytes 88
  379.3 10.8 %copy-start.16 = (s32[32]{0:T(128)S(1)}, s32[32]{0:T(128)}, u32[]{:S(2)}) copy-start(s32[32]{0:T(128)} %copy-done.15) | copy-start | bytes 388
  381.4 13.4 %copy-start.18 = (s32[11]{0:T(128)S(1)}, s32[11]{0:T(128)}, u32[]{:S(2)}) copy-start(s32[11]{0:T(128)} %copy-done.17) | copy-start | bytes 136
  384.8 5.0 collective-permute-start.12
  390.7 4.1 collective-permute-start.13
  405.5 10.0 %copy-start.6 = (f32[1,16,4,16,16]{1,2,4,3,0:T(4,128)S(1)}, f32[1,16,4,16,16]{1,2,4,3,0:T(4,128)}, u32[]{:S(2)}) copy-start(f32[1,16,4,16,16]{1,2,4,3,0:T(4,128)} %copy-done.5) | copy-start | bytes 196612
  409.7 114.9 %all-to-all-start.3 = ((f32[32,1,4096]{2,1,0:T(1,128)}), f32[32,1,4096]{2,1,0:T(1,128)S(1)}, u32[]{:S(2)}, u32[]{:S(2)}) async-start(f32[32,1,4096]{2,1,0:T(1,128)} %reshape.92), calls=%async_computation.3 | async-start | bytes 1048576 | tf_op jit(solution)/shard_map/all_to_all | solution.py:168
  415.4 177.4 %all-reduce.3.cloned.1.call-start = ((), (), s32[]{:S(2)}) async-start(), calls=%async_computation.4 | async-start | bytes 2097152 | tf_op jit(solution)/shard_map/psum | solution.py:205
  440.8 6.3 %copy-start.19 = (f32[16]{0:T(128)S(1)}, f32[16]{0:T(128)}, u32[]{:S(2)}) copy-start(f32[16]{0:T(128)} %get-tuple-element.27) | copy-start | bytes 196
  534.1 7.7 %copy-start.14 = (s32[19]{0:T(128)S(1)}, s32[19]{0:T(128)}, u32[]{:S(2)}) copy-start(s32[19]{0:T(128)} %copy-done.13) | copy-start | bytes 232
  536.9 0.8 copy-start.3
  536.9 4.9 collective-permute-start.14
  545.0 50.1 %collective-permute-start.15 = (f32[16,32,3,128]{3,1,2,0:T(8,128)}, f32[16,32,3,128]{3,1,2,0:T(8,128)}, u32[]{:S(2)}, u32[]{:S(2)}) collective-permute-start(f32[16,32,3,128]{3,1,2,0:T(8,128)} %slice.127), channel_id=1, source_target_pairs={{0,1},{1,2},{2,3},{3,4},{4,5},{5,6},{6,7},{7,8},{8,9},{9,10},{10,1... | collective-permute-start | bytes 2359304 | tf_op jit(solution)/shard_map/ppermute | solution.py:24
  595.1 1.8 copy-start.2
Sparse Core Ops, SparseCore 0:
  440.9 151.8 all-reduce.2
where the time goes:
time: 616 us; the launch traced here: 609 us
  waiting for transfers between devices  159 us (26%)
  blocking collectives  151 us (25%)
  local copies, waits for them, and re-layouts  122 us (20%)
  matrix products  119 us (19%)
  starting transfers between devices  29.7 us (5%)
  between operations  15.3 us (2%)
  other arithmetic  13.7 us (2%)
    ppermute x16, waiting for transfers between devices, from_behind(): lax.ppermute(value, axis, [(i, (i + by) % devices) for i in range(devices)])  106 us
    psum x1, blocking collectives, local(): point_total, bias_total = lax.psum((point_local, bias_local), ('gx', 'gy'))  77.5 us
    psum x1, waiting for transfers between devices, local(): mode_total = lax.psum(mode_local, 'gy')  41.4 us
    unnamed x56, local copies, waits for them, and re-layouts  40.1 us
    all_gather x2, blocking collectives, wave_block(): gathered = lax.all_gather(level_three, 'gx', axis=1, tiled=True)  31.6 us
    all_to_all x1, blocking collectives, wave_block(): lax.all_to_all(from_lanes(delta_one, channels), 'gy', split_axis=2, conca...  22 us
    dot_general x24, matrix products, plane_y(): jnp.einsum('kr,axr->axk', matrix, signal, precision=lax.Precision.HIGHEST)  20.3 us
    all_to_all x1, blocking collectives, wave_block(): lax.all_to_all(level_one, 'gy', split_axis=3, concat_axis=2, tiled=True)  19.5 us
  transfers between devices with their start and end apart: 19, of which 17 were waited for; matrix products, arithmetic and copies ran while one was open for 11% of the time, Pallas kernels for 0%

commit v1 on v0

--- a/solution.py
+++ b/solution.py
@@ -19,6 +19,12 @@
 GELU_CUBE = 0.044715
 
 
+def exchange_blocks(array, axis, split, join):
+    parts = jnp.split(array, lax.axis_size(axis), axis=split)
+    incoming = lax.all_to_all(jnp.stack(parts), axis, 0, 0)
+    return jnp.concatenate(incoming, axis=join)
+
+
 def from_behind(value, axis, by):
     devices = lax.axis_size(axis)
     return lax.ppermute(value, axis, [(i, (i + by) % devices) for i in range(devices)])
@@ -124,7 +130,7 @@
         filter_table(LOW_PASS, extent_y // 2, extent_y + 6, False),
         jnp.concatenate([halved, margin], 2),
     )
-    level_one = to_lanes(lax.all_to_all(level_one, "gy", split_axis=3, concat_axis=2, tiled=True))
+    level_one = to_lanes(exchange_blocks(level_one, "gy", 3, 2))
     rows_one, cols_one = (level_one.shape[1], level_one.shape[2])
     margin = from_behind(level_one[:, :6], "gx", -1)
     level_two = plane_x(

time: 616 us -> 710 us (1.15)
  local copies, waits for them, and re-layouts: 122 us -> 213 us
    unnamed x56 -> x108, local copies, waits for them, and re-layouts: 40.1 us -> 110 us
    another operation x0 -> x4, local copies, waits for them, and re-layouts: none -> 40.6 us  [exchange_blocks(): incoming = lax.all_to_all(jnp.stack(parts), axis, 0, 0)]
    all_to_all x3 -> x1, local copies, waits for them, and re-layouts: 10.1 us -> 0.51 us  [exchange_blocks(): incoming = lax.all_to_all(jnp.stack(parts), axis, 0, 0)]
    transpose x2 -> x0, local copies, waits for them, and re-layouts: 8.83 us -> none  [along_y(): jnp.einsum('kr,axrs->axks', matrix, signal, precision=lax.Precision.HIGHEST)]
  transfers between devices with their start and end apart: 19 -> 19, of which waited for: 17 -> 17; matrix products, arithmetic and copies ran while one was open for 11% -> 9% of each run, Pallas kernels for 0% -> 0%
where the time goes in v1:
time: 710 us; the launch traced here: 706 us
  local copies, waits for them, and re-layouts  213 us (30%)
  waiting for transfers between devices  159 us (22%)
  blocking collectives  150 us (21%)
  matrix products  123 us (17%)
  starting transfers between devices  30.2 us (4%)
  between operations  15.3 us (2%)
  other arithmetic  13.5 us (2%)
    unnamed x108, local copies, waits for them, and re-layouts  110 us
    ppermute x16, waiting for transfers between devices, from_behind(): lax.ppermute(value, axis, [(i, (i + by) % devices) for i in range(devices)])  107 us
    psum x1, blocking collectives, local(): point_total, bias_total = lax.psum((point_local, bias_local), ('gx', 'gy'))  77.5 us
    psum x1, waiting for transfers between devices, local(): mode_total = lax.psum(mode_local, 'gy')  41.3 us
    another operation x4, local copies, waits for them, and re-layouts, exchange_blocks(): incoming = lax.all_to_all(jnp.stack(parts), axis, 0, 0)  40.6 us
    all_gather x2, blocking collectives, wave_block(): gathered = lax.all_gather(level_three, 'gx', axis=1, tiled=True)  31.7 us
    all_to_all x1, blocking collectives, wave_block(): lax.all_to_all(from_lanes(delta_one, channels), 'gy', split_axis=2, conca...  22.1 us
    dot_general x24, matrix products, plane_y(): jnp.einsum('kr,axr->axk', matrix, signal, precision=lax.Precision.HIGHEST)  21 us
  transfers between devices with their start and end apart: 19, of which 17 were waited for; matrix products, arithmetic and copies ran while one was open for 9% of the time, Pallas kernels for 0%

profile of v1, /device:TPU:8, one launch (start us, length us, event | category | flops | bytes accessed | tf_op | source)
XLA Modules:
  0.0 705.6 jit_solution(13920406214901578323)
XLA Ops:
  9.3 6.7 collective-permute-done
  17.9 8.3 %collective-permute-start.1 = (f32[16,16,6,128]{3,1,2,0:T(8,128)S(1)}, f32[16,16,6,128]{3,1,2,0:T(8,128)S(1)}, u32[]{:S(2)}, u32[]{:S(2)}) collective-permute-start(f32[16,16,6,128]{3,1,2,0:T(8,128)S(1)} %slice.105), channel_id=1, source_target_pairs={{0,31},{1,0},{2,1},{3,2},{4,3},{5,4},{6,5},{7,6},{8,7},{9,8},{10,9... | collective-permute-start | bytes 2359304 | tf_op jit(solution)/shard_map/ppermute | solution.py:30
  26.2 17.1 %collective-permute-done.1 = f32[16,16,6,128]{3,1,2,0:T(8,128)S(1)} collective-permute-done((f32[16,16,6,128]{3,1,2,0:T(8,128)S(1)}, f32[16,16,6,128]{3,1,2,0:T(8,128)S(1)}, u32[]{:S(2)}, u32[]{:S(2)}) %collective-permute-start.1) | collective-permute-done | bytes 786464 | tf_op jit(solution)/shard_map/ppermute | solution.py:30
  81.7 19.2 %copy.267 = f32[32,16,16,4,4]{2,1,4,3,0:T(8,128)} copy(f32[32,16,16,4,4]{4,3,2,1,0:T(4,128)} %fusion.94) | data formatting | bytes 1048576 | tf_op jit(solution)/shard_map/stack | solution.py:24
  100.9 4.2 reshape.102
  105.1 7.5 %all-to-all-start = ((f32[32,1,4096]{2,1,0:T(1,128)}), f32[32,1,4096]{2,1,0:T(1,128)S(1)}, u32[]{:S(2)}, u32[]{:S(2)}) async-start(f32[32,1,4096]{2,1,0:T(1,128)} %reshape.102), calls=%async_computation | async-start | bytes 1048576 | tf_op jit(solution)/shard_map/all_to_all | solution.py:24
  112.6 6.2 copy.356
  118.8 11.5 %all-to-all-done = f32[32,1,4096]{2,1,0:T(1,128)S(1)} async-done(((f32[32,1,4096]{2,1,0:T(1,128)}), f32[32,1,4096]{2,1,0:T(1,128)S(1)}, u32[]{:S(2)}, u32[]{:S(2)}) %all-to-all-start) | async-done | bytes 524320 | tf_op jit(solution)/shard_map/all_to_all | solution.py:24
  135.4 3.7 copy.268
  139.2 3.9 collective-permute-done.2
  146.1 3.9 collective-permute-done.3
  151.0 14.5 %all_gather.6 = f32[64,32,32]{0,2,1:T(8,128)S(1)} all-gather(f32[64,4,32]{0,2,1:T(8,128)S(1)} %fusion.187), channel_id=1, replica_groups=mesh['gx'=8,'gy'=32] {'gx'}, dimensions={1}, use_global_device_ids=true | all-gather | bytes 294912 | tf_op jit(solution)/shard_map/all_gather | solution.py:148
  171.9 14.6 %bitcast_subtract_fusion.1 = f32[4,16,4,16,16]{1,2,4,3,0:T(4,128)S(1)} fusion(f32[4,16,16,16,16]{2,1,4,3,0:T(8,128)} %bitcast.516, f32[1,16,4,16,16]{1,2,4,3,0:T(4,128)S(1)} %copy.283, f32[1,16,4,16,16]{1,2,4,3,0:T(4,128)S(1)} %copy.282, f32[1,16,4,16,16]{1,2,4,3,0:T(4,128)S(1)} %copy.281, f32[1,16,4,16,16]{1,2,4,3,0:T(4,128)S(1)} %copy.280), kind=kOutput, calls=%fused_computation.23 | convolution fusion | flops 13041664 | bytes 1572864 | tf_op jit(solution)/shard_map/bizxy,bioxy->bozxy/dot_general | solution.py:157
  197.0 4.8 collective-permute-done.4
  202.7 4.0 collective-permute-done.5
  208.3 4.4 copy.297
  212.8 4.9 bitcast_bitcast_fusion.1
  217.6 3.5 reshape.104
  221.1 22.1 %all_to_all.46 = f32[32,1,4096]{2,1,0:T(1,128)S(1)} all-to-all(f32[32,1,4096]{2,1,0:T(1,128)S(1)} %reshape.104), channel_id=1, replica_groups=mesh['gx'=8,'gy'=32] {'gy'}, dimensions={0} | all-to-all | bytes 1048576 | tf_op jit(solution)/shard_map/all_to_all | solution.py:174
  247.9 4.8 copy.298
  255.6 4.4 collective-permute-done.6
  266.2 15.1 %collective-permute-done.7 = f32[16,32,3,128]{3,1,2,0:T(8,128)S(1)} collective-permute-done((f32[16,32,3,128]{3,1,2,0:T(8,128)S(1)}, f32[16,32,3,128]{3,1,2,0:T(8,128)S(1)}, u32[]{:S(2)}, u32[]{:S(2)}) %collective-permute-start.7) | collective-permute-done | bytes 786464 | tf_op jit(solution)/shard_map/ppermute | solution.py:30
  281.4 8.0 %fusion.1197 = (f32[16]{0:T(128)}, f32[16,32,8,128]{3,2,1,0:T(8,128)S(1)}, f32[16,32,8,128]{3,2,1,0:T(8,128)}) fusion(f32[16,32,8,128]{3,2,1,0:T(8,128)} %param.6, f32[16]{0:T(128)S(1)} %copy-done.16, f32[16,32,8,128]{3,0,2,1:T(8,128)S(1)} %fusion.27, f32[16,32,8,128]{3,2,1,0:T(8,128)} %param.5, s32[7]{0:T(128)S(1)} %iota_multiply_fusion.2, ...), kind=kOutput, calls=%fused_computation.1326 | convolution fusion | flops 56100200 | bytes 12320924 | tf_op jit(solution)/shard_map/kr,axrs->axks/dot_general | solution.py:60
  289.5 5.3 collective-permute-done.8
  297.5 19.6 %collective-permute-done.9 = f32[16,16,6,128]{3,1,2,0:T(8,128)S(1)} collective-permute-done((f32[16,16,6,128]{3,1,2,0:T(8,128)S(1)}, f32[16,16,6,128]{3,1,2,0:T(8,128)S(1)}, u32[]{:S(2)}, u32[]{:S(2)}) %collective-permute-start.9) | collective-permute-done | bytes 786464 | tf_op jit(solution)/shard_map/ppermute | solution.py:30
  355.6 19.2 %copy.307 = f32[32,16,16,4,4]{2,1,4,3,0:T(8,128)} copy(f32[32,16,16,4,4]{4,3,2,1,0:T(4,128)} %fusion.62) | data formatting | bytes 1048576 | tf_op jit(solution)/shard_map/stack | solution.py:24
  374.8 3.5 reshape.106
  378.3 19.3 %all_to_all.47 = f32[32,1,4096]{2,1,0:T(1,128)S(1)} all-to-all(f32[32,1,4096]{2,1,0:T(1,128)S(1)} %reshape.106), channel_id=1, replica_groups=mesh['gx'=8,'gy'=32] {'gy'}, dimensions={0} | all-to-all | bytes 1048576 | tf_op jit(solution)/shard_map/all_to_all | solution.py:24
  402.2 3.7 copy.308
  406.0 3.9 collective-permute-done.10
  412.9 5.2 collective-permute-done.11
  419.1 17.2 %all_gather.7 = f32[64,32,32]{0,2,1:T(8,128)S(1)} all-gather(f32[64,4,32]{0,2,1:T(8,128)S(1)} %fusion.183), channel_id=1, replica_groups=mesh['gx'=8,'gy'=32] {'gx'}, dimensions={1}, use_global_device_ids=true | all-gather | bytes 294912 | tf_op jit(solution)/shard_map/all_gather | solution.py:148
  444.2 18.0 %bitcast_subtract_fusion = f32[4,16,4,16,16]{1,2,4,3,0:T(4,128)S(1)} fusion(f32[4,16,16,16,16]{2,1,4,3,0:T(8,128)} %bitcast.517, f32[1,16,4,16,16]{1,2,4,3,0:T(4,128)} %copy.323, f32[1,16,4,16,16]{1,2,4,3,0:T(4,128)} %copy.322, f32[1,16,4,16,16]{1,2,4,3,0:T(4,128)} %copy.321, f32[1,16,4,16,16]{1,2,4,3,0:T(4,128)S(1)} %copy.320), kind=kOutput, calls=%fused_computation.19 | convolution fusion | flops 13041664 | bytes 1572864 | tf_op jit(solution)/shard_map/bozxy,bioxy->bizxy/dot_general | solution.py:153
  478.5 4.8 collective-permute-done.12
  485.5 4.0 collective-permute-done.13
  491.7 4.4 copy.337
  496.2 4.7 bitcast_bitcast_fusion
  500.9 4.2 reshape.108
  505.1 5.7 all-to-all-start.3
  510.9 17.6 %fusion.150 = f32[4,16,16,16,16]{4,3,2,1,0:T(8,128)} fusion(f32[1,16,4,16,16]{1,2,4,3,0:T(4,128)} %copy.323, f32[1,16,4,16,16]{1,2,4,3,0:T(4,128)} %copy.322, f32[1,16,4,16,16]{1,2,4,3,0:T(4,128)} %copy.321, f32[1,16,4,16,16]{1,2,4,3,0:T(4,128)} %copy-done.8, f32[1,16,4,16,16]{1,2,4,3,0:T(4,128)} %copy-done.7, f32[1,16,4,16,16]{1,2,4,3,0:T(4,128)} %copy-done.5, ...), kind=kOutput, calls=%fused_computation.234 | convolution fusion | flops 12976128 | bytes 1572864 | tf_op jit(solution)/shard_map/bizxy,bozxy->bioxy/dot_general | solution.py:207
  528.4 7.6 %copy.344 = f32[4,16,16,256]{3,2,1,0:T(8,128)} copy(f32[4,16,16,256]{1,2,3,0:T(8,128)} %bitcast.518) | data formatting | bytes 2097152 | tf_op jit(solution)/shard_map/reshape | solution.py:210
  536.0 6.3 fusion.45
  542.3 77.5 %all-reduce = (f32[16,16]{0,1:T(8,128)S(1)}, f32[16]{0:T(128)S(1)}) all-reduce(f32[16,16]{0,1:T(8,128)S(1)} %fusion.45, f32[16]{0:T(128)S(1)} %copy-done.15), channel_id=1, replica_groups=mesh['gx'=8,'gy'=32] {'gx','gy'}, use_global_device_ids=true, to_apply=%region_1.2 | all-reduce | flops 272 | bytes 2176 | tf_op jit(solution)/shard_map/psum | solution.py:216
  624.5 4.8 copy.338
  632.8 4.1 collective-permute-done.14
  642.2 4.4 fusion.24
  646.6 41.3 %all-reduce.3.cloned.1.call-done = f32[4,16,16,256]{3,2,1,0:T(8,128)} async-done(((f32[4,16,16,256]{3,2,1,0:T(8,128)}), f32[4,16,16,256]{3,2,1,0:T(8,128)}) %all-reduce.3.cloned.1.call-update) | async-done | bytes 1048592 | tf_op jit(solution)/shard_map/psum | solution.py:211
  691.6 6.9 bitcast_add_fusion
  (237 shorter events, 180.3 us)
Async XLA Ops:
  7.2 256.2 %copy-start = (f32[16,16]{1,0:T(8,128)S(1)}, f32[16,16]{1,0:T(8,128)}, u32[]{:S(2)}) copy-start(f32[16,16]{1,0:T(8,128)} %param.8) | copy-start | bytes 3076
  9.2 6.7 collective-permute-start
  17.9 25.4 %collective-permute-start.1 = (f32[16,16,6,128]{3,1,2,0:T(8,128)S(1)}, f32[16,16,6,128]{3,1,2,0:T(8,128)S(1)}, u32[]{:S(2)}, u32[]{:S(2)}) collective-permute-start(f32[16,16,6,128]{3,1,2,0:T(8,128)S(1)} %slice.105), channel_id=1, source_target_pairs={{0,31},{1,0},{2,1},{3,2},{4,3},{5,4},{6,5},{7,6},{8,7},{9,8},{10,9... | collective-permute-start | bytes 2359304 | tf_op jit(solution)/shard_map/ppermute | solution.py:30
  74.9 37.7 %copy-start.3 = (f32[4,16,16,256]{3,2,1,0:T(8,128)S(1)}, f32[4,16,16,256]{3,2,1,0:T(8,128)}, u32[]{:S(2)}) copy-start(f32[4,16,16,256]{3,2,1,0:T(8,128)} %param.7) | copy-start | bytes 3145732
  105.1 25.1 %all-to-all-start = ((f32[32,1,4096]{2,1,0:T(1,128)}), f32[32,1,4096]{2,1,0:T(1,128)S(1)}, u32[]{:S(2)}, u32[]{:S(2)}) async-start(f32[32,1,4096]{2,1,0:T(1,128)} %reshape.102), calls=%async_computation | async-start | bytes 1048576 | tf_op jit(solution)/shard_map/all_to_all | solution.py:24
  139.2 3.9 collective-permute-start.2
  144.2 5.8 collective-permute-start.3
  146.1 272.5 %copy-start.13 = (s32[32]{0:T(128)}, s32[32]{0:T(128)S(1)}, u32[]{:S(2)}) copy-start(s32[32]{0:T(128)S(1)} %iota_multiply_fusion.3) | copy-start | bytes 388
  169.1 2.0 copy-start.4
  169.7 1.3 copy-start.5
  170.4 0.8 copy-start.6
  171.1 0.9 copy-start.7
  196.8 5.0 collective-permute-start.4
  197.0 84.5 %copy-start.9 = (s32[7]{0:T(128)}, s32[7]{0:T(128)S(1)}, u32[]{:S(2)}) copy-start(s32[7]{0:T(128)S(1)} %iota_multiply_fusion.2) | copy-start | bytes 88
  202.7 4.1 collective-permute-start.5
  202.7 49.9 %copy-start.14 = (s32[11]{0:T(128)}, s32[11]{0:T(128)S(1)}, u32[]{:S(2)}) copy-start(s32[11]{0:T(128)S(1)} %iota_multiply_fusion.1) | copy-start | bytes 136
  212.8 50.6 %copy-start.1 = (f32[16,32,8,128]{3,2,1,0:T(8,128)S(1)}, f32[16,32,8,128]{3,2,1,0:T(8,128)}, u32[]{:S(2)}) copy-start(f32[16,32,8,128]{3,2,1,0:T(8,128)} %param.5) | copy-start | bytes 6291460
  221.1 60.3 %copy-start.16 = (f32[16]{0:T(128)S(1)}, f32[16]{0:T(128)}, u32[]{:S(2)}) copy-start(f32[16]{0:T(128)} %param.9) | copy-start | bytes 196
  255.5 4.4 collective-permute-start.6
  255.5 41.4 %copy-start.11 = (s32[19]{0:T(128)}, s32[19]{0:T(128)S(1)}, u32[]{:S(2)}) copy-start(s32[19]{0:T(128)S(1)} %iota_multiply_fusion) | copy-start | bytes 232
  261.1 20.2 %collective-permute-start.7 = (f32[16,32,3,128]{3,1,2,0:T(8,128)S(1)}, f32[16,32,3,128]{3,1,2,0:T(8,128)S(1)}, u32[]{:S(2)}, u32[]{:S(2)}) collective-permute-start(f32[16,32,3,128]{3,1,2,0:T(8,128)S(1)} %slice.115), channel_id=1, source_target_pairs={{0,1},{1,2},{2,3},{3,4},{4,5},{5,6},{6,7},{7,8},{8,9},{9,10},{10,1... | collective-permute-start | bytes 2359304 | tf_op jit(solution)/shard_map/ppermute | solution.py:30
  289.4 5.3 collective-permute-start.8
  297.0 20.1 %collective-permute-start.9 = (f32[16,16,6,128]{3,1,2,0:T(8,128)S(1)}, f32[16,16,6,128]{3,1,2,0:T(8,128)S(1)}, u32[]{:S(2)}, u32[]{:S(2)}) collective-permute-start(f32[16,16,6,128]{3,1,2,0:T(8,128)S(1)} %slice.117), channel_id=1, source_target_pairs={{0,31},{1,0},{2,1},{3,2},{4,3},{5,4},{6,5},{7,6},{8,7},{9,8},{10,9... | collective-permute-start | bytes 2359304 | tf_op jit(solution)/shard_map/ppermute | solution.py:30
  406.0 3.9 collective-permute-start.10
  411.0 7.1 %collective-permute-start.11 = (f32[64,6,64]{2,1,0:T(8,128)S(1)}, f32[64,6,64]{2,1,0:T(8,128)S(1)}, u32[]{:S(2)}, u32[]{:S(2)}) collective-permute-start(f32[64,6,64]{2,1,0:T(8,128)S(1)} %bitcast.542), channel_id=1, source_target_pairs={{0,224},{32,0},{64,32},{96,64},{128,96},{160,128},{192,160},{224,1... | collective-permute-start | bytes 294920 | tf_op jit(solution)/shard_map/ppermute | solution.py:30
  439.9 4.3 copy-start.8
  478.3 5.0 collective-permute-start.12
  485.5 4.1 collective-permute-start.13
  500.9 41.4 %copy-start.15 = (f32[16]{0:T(128)S(1)}, f32[16]{0:T(128)}, u32[]{:S(2)}) copy-start(f32[16]{0:T(128)} %get-tuple-element.27) | copy-start | bytes 196
  505.1 114.7 %all-to-all-start.3 = ((f32[32,1,4096]{2,1,0:T(1,128)}), f32[32,1,4096]{2,1,0:T(1,128)S(1)}, u32[]{:S(2)}, u32[]{:S(2)}) async-start(f32[32,1,4096]{2,1,0:T(1,128)} %reshape.108), calls=%async_computation.3 | async-start | bytes 1048576 | tf_op jit(solution)/shard_map/all_to_all | solution.py:174
  510.8 177.1 %all-reduce.3.cloned.1.call-start = ((), (), s32[]{:S(2)}) async-start(), calls=%async_computation.4 | async-start | bytes 2097152 | tf_op jit(solution)/shard_map/psum | solution.py:211
  528.4 108.6 %copy-start.12 = (s32[19]{0:T(128)S(1)}, s32[19]{0:T(128)}, u32[]{:S(2)}) copy-start(s32[19]{0:T(128)} %copy-done.11) | copy-start | bytes 232
  542.3 149.3 %copy-start.10 = (s32[7]{0:T(128)S(1)}, s32[7]{0:T(128)}, u32[]{:S(2)}) copy-start(s32[7]{0:T(128)} %copy-done.9) | copy-start | bytes 88
  632.0 0.8 copy-start.2
  632.1 4.9 collective-permute-start.14
  640.1 50.1 %collective-permute-start.15 = (f32[16,32,3,128]{3,1,2,0:T(8,128)}, f32[16,32,3,128]{3,1,2,0:T(8,128)}, u32[]{:S(2)}, u32[]{:S(2)}) collective-permute-start(f32[16,32,3,128]{3,1,2,0:T(8,128)} %slice.127), channel_id=1, source_target_pairs={{0,1},{1,2},{2,3},{3,4},{4,5},{5,6},{6,7},{7,8},{8,9},{9,10},{10,1... | collective-permute-start | bytes 2359304 | tf_op jit(solution)/shard_map/ppermute | solution.py:30
Sparse Core Ops, SparseCore 0:
  536.1 151.7 all-reduce.2
